TPU v7x, 32 devices: a whole 2x2x4 slice. The times are simulated.
32 devices in a mesh: groups: 2 (over x), sect: 8 (over z, y), head: 2 (over core).
Axes of the slice: x: 2, y: 2, z: 4, core: 2. Of those that a mesh axis runs over, the one named last changes fastest.
Arguments:
- queries: bfloat16 [2048, 8192], P(('groups', 'sect'), 'head'), parts along dimension 0, may hold values from -200 to 200
- packed_key_rows: bfloat16 [2048, 512], P(('groups', 'sect'), 'head'), parts along dimension 0, may hold values from -7 to 7
- values: bfloat16 [2048, 512], P(('groups', 'sect'), 'head'), parts along dimension 0, may hold values from -12 to 12
- segments: int32 [2048], P('groups'), parts along dimension 0, may hold values from 0 to 7, never falling along the last dimension, each value on 1 to 512 neighbouring positions
- proj_weight: bfloat16 [8192, 2048], P('head', 'sect'), may hold values from -0.0625 to 0.0625
- residual: bfloat16 [2048, 2048], P(('groups', 'sect', 'head')), parts along dimension 0, may hold values from -2 to 2
- norm_gain: bfloat16 [2048], replicated, may hold values from 0.5 to 1.5
- expert_ids: int32 [2048, 8], P(('groups', 'sect', 'head')), parts along dimension 0, may hold values from 0 to 15, all different within a row; in each aligned block of 64 rows (0 to 63, 64 to 127, ...) at most 48 rows name the same one
- route_weights: float32 [2048, 8], P(('groups', 'sect', 'head')), parts along dimension 0, may hold values from 0.05 to 1
- gate_weight: bfloat16 [16, 2048, 768], P(('sect', 'head')), may hold values from -0.125 to 0.125
- up_weight: bfloat16 [16, 2048, 768], P(('sect', 'head')), may hold values from -0.125 to 0.125
- down_weight: bfloat16 [16, 768, 2048], P(('sect', 'head')), may hold values from -0.21875 to 0.21875
Outputs:
- hidden_mid: bfloat16 [2048, 2048], P(('groups', 'sect', 'head')), parts along dimension 0
- expert_mix: bfloat16 [2048, 2048], P(('groups', 'sect', 'head')), parts along dimension 0
There are 2 independent parts, one for each index of `groups`. A program takes and returns all parts, laid end to end along the dimension named above; an argument that names none is the same for every part. Nothing has to cross between parts.
Inputs may be any that keep to these rules, and one draw needn't show every extreme that they name: `segments`: ids never fall along the rows; each of the 8 prompts has 1 to 512 rows, and one has exactly that many. `expert_ids`: each row names 8 different experts. Within the rows of one device (aligned blocks of 64 rows) no expert is named by more than 48 rows.
All inputs are finite; a program needn't handle non-finite values.
Results may differ from a plain program's by a relative error of at most 0.02.
Values may be sent and summed in bfloat16 or wider, within the bound.
A program may use at most 256 MiB of HBM per device.

v0:
```python
import functools
import math

import jax
import jax.numpy as jnp
from jax import lax
from jax.experimental import pallas as pl
from jax.experimental.pallas import tpu as pltpu
from jax.sharding import PartitionSpec as P

HEAD_WIDTH = 128
MASKED = -1e30
NORM_EPS = 1e-06
VMEM_ROOM = 64 << 20
LAYER_ROOM = 52 << 20

MESH = pl.DeviceIdType.MESH
VMEM_SPEC = pl.BlockSpec(memory_space=pltpu.VMEM)
ANY_SPEC = pl.BlockSpec(memory_space=pl.ANY)
DMA = pltpu.SemaphoreType.DMA

def greet(devices):
    barrier = pltpu.get_barrier_semaphore()
    for device in devices:
        pl.semaphore_signal(barrier, inc=1, device_id=device, device_id_type=MESH)
    pl.semaphore_wait(barrier, len(devices))

def remote(src, dst, send_sem, recv_sem, device):
    return pltpu.make_async_remote_copy(
        src_ref=src,
        dst_ref=dst,
        send_sem=send_sem,
        recv_sem=recv_sem,
        device_id=device,
        device_id_type=MESH,
    )

def attention_body(
    extra,
    groups,
    sects,
    kv_heads,
    q_ref,
    k_ref,
    v_ref,
    seg_ref,
    w_ref,
    a_out,
    w_out,
    kv_ref,
    kv_all,
    att,
    bias,
    kz_send,
    kz_recv,
    ky_send,
    ky_recv,
    a_send,
    a_recv,
    w_send,
    w_recv,
    f_send,
    f_recv,
    local_sem,
):
    g = lax.axis_index("groups")
    s = lax.axis_index("sect")
    halves = sects // 2
    h = s // 2
    low = lax.rem(s, 2)
    rows = q_ref.shape[0]
    cols = q_ref.shape[1] // sects
    w_cols = w_ref.shape[1]
    w_rows = w_ref.shape[0] // sects
    part = w_rows // groups
    other_y = 2 * h + 1 - low
    sect_peers = [lax.rem(s + i, sects) for i in range(1, sects)]
    group_peers = [lax.rem(g + i, groups) for i in range(1, groups)]
    half = k_ref.shape[1]
    own_k = pltpu.make_async_copy(k_ref, kv_ref.at[:, pl.ds(0, half)], local_sem.at[3])
    own_v = pltpu.make_async_copy(v_ref, kv_ref.at[:, pl.ds(half, half)], local_sem.at[4])
    own_k.start()
    own_v.start()
    greet(
        [{"sect": t} for t in sect_peers] + [{"groups": t} for t in group_peers] + extra
    )
    started = []
    own_k.wait()
    own_v.wait()

    def kv_cross(t):
        return remote(
            kv_ref if t is None else kv_all.at[2 * t + low],
            kv_all.at[s if t is None else 2 * t + low],
            ky_send.at[h if t is None else t],
            ky_recv.at[h if t is None else t],
            {"sect": other_y},
        )

    for i in range(1, halves):
        t = lax.rem(h + i, halves)
        copy = remote(
            kv_ref, kv_all.at[s], kz_send.at[t], kz_recv.at[h], {"sect": 2 * t + low}
        )
        copy.start()
        started.append(copy)
    copy = kv_cross(None)
    copy.start()
    started.append(copy)
    own_kv = pltpu.make_async_copy(kv_ref, kv_all.at[s], local_sem.at[0])
    own_kv.start()

    def w_piece(t):
        return w_ref.at[pl.ds(pl.multiple_of(t * w_rows + g * part, part), part), :]

    def w_place(group, t):
        span = pl.ds(pl.multiple_of(group * part, part), part)
        if len(w_out.shape) == 3:
            return w_out.at[t, span, :]
        return w_out.at[span, pl.ds(pl.multiple_of(t * w_cols, w_cols), w_cols)]

    for t in sect_peers:
        copy = remote(
            w_piece(t), w_place(g, s), w_send.at[t], w_recv.at[s], {"sect": t}
        )
        copy.start()
        started.append(copy)
    own_w = pltpu.make_async_copy(w_piece(s), w_place(g, s), local_sem.at[1])
    own_w.start()
    for i, t in enumerate(group_peers):
        copy = remote(
            w_piece(s), w_place(g, s), f_send.at[i, s], f_recv.at[g, s], {"groups": t}
        )
        copy.start()
        started.append(copy)

    for i in range(1, halves):
        t = lax.rem(h + i, halves)
        remote(
            kv_ref, kv_all.at[2 * t + low], kz_send.at[t], kz_recv.at[t], {"sect": 2 * t + low}
        ).wait_recv()
        copy = kv_cross(t)
        copy.start()
        started.append(copy)

    window = bias.shape[1]
    blocks = window // rows
    first = jnp.maximum(s - (blocks - 1), 0)
    row_of = lax.broadcasted_iota(jnp.int32, (rows, rows), 0)
    col_of = lax.broadcasted_iota(jnp.int32, (rows, rows), 1)
    seg_q = jnp.sum(
        jnp.where(row_of == col_of, seg_ref[s].astype(jnp.float32), 0.0), axis=1, keepdims=True
    )
    for b in range(blocks):
        behind = (s - first - b) * rows + row_of - col_of
        same = seg_q == seg_ref[first + b].astype(jnp.float32)
        bias[:, b * rows : (b + 1) * rows] = jnp.where(
            jnp.logical_and(same, behind >= 0), 0.0, MASKED
        )

    for i in range(halves):
        t = lax.rem(h + i, halves)
        remote(
            kv_ref, kv_all.at[2 * t + 1 - low], ky_send.at[t], ky_recv.at[t], {"sect": other_y}
        ).wait_recv()
    own_kv.wait()

    scale = 1.0 / math.sqrt(HEAD_WIDTH)
    kv_width = kv_heads * HEAD_WIDTH
    per_kv = q_ref.shape[1] // kv_heads

    def attend(i, carry):
        t = lax.rem(s + 1 + i, sects)
        kv_head = (t * cols) // per_kv
        k_col = pl.multiple_of(kv_head * HEAD_WIDTH, HEAD_WIDTH)
        v_col = pl.multiple_of(kv_width + kv_head * HEAD_WIDTH, HEAD_WIDTH)
        span = pl.ds(first, blocks)
        keys = kv_all[span, :, pl.ds(k_col, HEAD_WIDTH)].reshape(window, HEAD_WIDTH)
        vals = kv_all[span, :, pl.ds(v_col, HEAD_WIDTH)].reshape(window, HEAD_WIDTH)
        for j in range(cols // HEAD_WIDTH):
            q_col = pl.multiple_of(t * cols + j * HEAD_WIDTH, HEAD_WIDTH)
            q = q_ref[:, pl.ds(q_col, HEAD_WIDTH)]
            scores = lax.dot_general(
                q, keys, (((1,), (1,)), ((), ())), preferred_element_type=jnp.float32
            )
            scores = scores * scale + bias[...]
            top = jnp.max(scores, axis=1, keepdims=True)
            weights = jnp.exp(scores - top).astype(jnp.bfloat16)
            total = jnp.sum(weights.astype(jnp.float32), axis=1, keepdims=True)
            mixed = jnp.dot(weights, vals, preferred_element_type=jnp.float32)
            att[t, :, j * HEAD_WIDTH : (j + 1) * HEAD_WIDTH] = (mixed / total).astype(
                jnp.bfloat16
            )
        return carry

    def a_place(t):
        return a_out.at[pl.ds(pl.multiple_of(t * rows, rows), rows), :]

    def a_copy(t):
        return remote(att.at[t], a_place(s), a_send.at[t], a_recv.at[s], {"sect": t})

    def step(i, carry):
        attend(i, carry)

        @pl.when(i >= 1)
        def _():
            a_copy(lax.rem(s + i, sects)).start()

        return carry

    lax.fori_loop(0, sects, step, 0)
    own_a = pltpu.make_async_copy(att.at[s], a_place(s), local_sem.at[2])
    own_a.start()

    for t in sect_peers:
        remote(
            w_piece(s), w_place(g, t), w_send.at[t], w_recv.at[t], {"sect": t}
        ).wait_recv()
        for i, u in enumerate(group_peers):
            copy = remote(
                w_place(g, t), w_place(g, t), f_send.at[i, t], f_recv.at[g, t], {"groups": u}
            )
            copy.start()
            started.append(copy)

    def wait_rows(t):
        remote(att.at[t], a_place(t), a_send.at[t], a_recv.at[t], {"sect": t}).wait_recv()

    def wait_weight():
        for u in group_peers:
            for t in [s] + sect_peers:
                remote(
                    w_place(g, t),
                    w_place(u, t),
                    f_send.at[0, t],
                    f_recv.at[u, t],
                    {"groups": u},
                ).wait_recv()
        own_w.wait()

    def drain():
        for copy in started:
            copy.wait_send()
        for t in sect_peers:
            a_copy(t).wait_send()

    return sect_peers, wait_rows, wait_weight, own_a.wait, drain

def attention_kernel(*arguments):
    sect_peers, wait_rows, wait_weight, wait_own, drain = attention_body([], *arguments)
    for t in sect_peers:
        wait_rows(t)
    wait_weight()
    wait_own()
    drain()

def attention_scratch(groups, sects, rows, cols, kv_shape, window):
    return [
        pltpu.VMEM(kv_shape, jnp.bfloat16),
        pltpu.VMEM((sects,) + kv_shape, jnp.bfloat16),
        pltpu.VMEM((sects, rows, cols), jnp.bfloat16),
        pltpu.VMEM((rows, window), jnp.float32),
        DMA((sects // 2,)),
        DMA((sects // 2,)),
        DMA((sects // 2,)),
        DMA((sects // 2,)),
        DMA((sects,)),
        DMA((sects,)),
        DMA((sects,)),
        DMA((sects,)),
        DMA((groups, sects)),
        DMA((groups, sects)),
        DMA((5,)),
    ]

def exchange_attention(queries, keys, values, segments, proj_weight):
    kv_heads = keys.shape[1] // HEAD_WIDTH
    groups = lax.axis_size("groups")
    sects = lax.axis_size("sect")
    rows, width = queries.shape
    cols = width // sects
    w_rows = proj_weight.shape[0] // sects
    w_cols = proj_weight.shape[1]
    blocks = min(sects, -(-segments.shape[0] // (2 * rows)) + 1)
    kv_shape = (rows, 2 * keys.shape[1])
    aligned = w_cols % 128 == 0
    w_shape = (w_rows, w_cols * sects) if aligned else (sects, w_rows, w_cols)
    attended, weight = pl.pallas_call(
        functools.partial(attention_kernel, groups, sects, kv_heads),
        out_shape=(
            jax.ShapeDtypeStruct((rows * sects, cols), jnp.bfloat16),
            jax.ShapeDtypeStruct(w_shape, jnp.bfloat16),
        ),
        in_specs=[VMEM_SPEC, VMEM_SPEC, VMEM_SPEC, VMEM_SPEC, ANY_SPEC],
        out_specs=(ANY_SPEC, ANY_SPEC),
        scratch_shapes=attention_scratch(groups, sects, rows, cols, kv_shape, blocks * rows),
        compiler_params=pltpu.CompilerParams(collective_id=0, has_side_effects=True),
        name="attention",
    )(queries, keys, values, segments.reshape(sects, 1, rows), proj_weight)
    if not aligned:
        weight = weight.transpose(1, 0, 2).reshape(w_rows, w_cols * sects)
    return attended, weight

def positions():
    s = lax.axis_index("sect")
    c = lax.axis_index("head")
    halves = lax.axis_size("sect") // 2
    h = s // 2
    low = lax.rem(s, 2)
    partner = {"head": 1 - c}
    across = {"sect": 2 * h + 1 - low}
    others = [lax.rem(h + i, halves) for i in range(1, halves)]
    return s, c, h, low, halves, partner, across, others

def sum_kernel(
    p_ref, o_ref, rp, cs, ry, zs, rz, p_send, p_recv, y_send, y_recv, z_send, z_recv
):
    s, c, h, low, halves, partner, across, others = positions()
    greet([partner, across] + [{"sect": 2 * t + low} for t in others])
    order = others + [h]
    started = []

    def widen(x):
        return x.astype(jnp.float32)

    for t in order:
        copy = remote(
            p_ref.at[pl.ds(2 * t, 2), 1 - c], rp.at[t], p_send.at[t], p_recv.at[t], partner
        )
        copy.start()
        started.append(copy)
    for t in order:
        remote(
            p_ref.at[pl.ds(2 * t, 2), 1 - c], rp.at[t], p_send.at[t], p_recv.at[t], partner
        ).wait_recv()
        cs[t] = (widen(p_ref[2 * t + 1 - low, c]) + widen(rp[t, 1 - low])).astype(jnp.bfloat16)
        copy = remote(cs.at[t], ry.at[t], y_send.at[t], y_recv.at[t], across)
        copy.start()
        started.append(copy)
    for t in order:
        remote(cs.at[t], ry.at[t], y_send.at[t], y_recv.at[t], across).wait_recv()
        total = widen(p_ref[2 * t + low, c]) + widen(rp[t, low]) + widen(ry[t])
        if t is h:
            o_ref[...] = total
        else:
            zs[t] = total.astype(jnp.bfloat16)
            copy = remote(
                zs.at[t], rz.at[h], z_send.at[t], z_recv.at[h], {"sect": 2 * t + low}
            )
            copy.start()
            started.append(copy)
    for t in others:
        remote(
            zs.at[t], rz.at[t], z_send.at[t], z_recv.at[t], {"sect": 2 * t + low}
        ).wait_recv()
        o_ref[...] += widen(rz[t])
    for copy in started:
        copy.wait_send()

def sum_scatter(partial_rows, moe_rows, collective_id):
    sects = lax.axis_size("sect")
    heads = lax.axis_size("head")
    width = partial_rows.shape[1]
    halves = sects // 2
    block = (moe_rows, width)
    return pl.pallas_call(
        sum_kernel,
        out_shape=jax.ShapeDtypeStruct(block, jnp.float32),
        in_specs=[VMEM_SPEC],
        out_specs=VMEM_SPEC,
        scratch_shapes=[
            pltpu.VMEM((halves, 2) + block, jnp.bfloat16),
            pltpu.VMEM((halves,) + block, jnp.bfloat16),
            pltpu.VMEM((halves,) + block, jnp.bfloat16),
            pltpu.VMEM((halves,) + block, jnp.bfloat16),
            pltpu.VMEM((halves,) + block, jnp.bfloat16),
        ]
        + [DMA((halves,))] * 6,
        compiler_params=pltpu.CompilerParams(
            collective_id=collective_id, has_side_effects=True
        ),
        name="sum_scatter",
    )(partial_rows.reshape((sects, heads) + block))

def gather_kernel(
    x_ref, o_ref, p_send, p_recv, y_send, y_recv, z_send, z_recv, local_sem
):
    s, c, h, low, halves, partner, across, others = positions()
    greet([partner, across] + [{"sect": 2 * t + low} for t in others])
    started = []

    def send(src, row, send_sem, recv_sem, device):
        copy = remote(src, o_ref.at[row, c], send_sem, recv_sem, device)
        copy.start()
        started.append(copy)

    for t in others:
        send(x_ref, s, z_send.at[t], z_recv.at[h], {"sect": 2 * t + low})
    send(x_ref, s, y_send.at[h], y_recv.at[h], across)
    send(x_ref, s, p_send.at[s], p_recv.at[s], partner)
    own = pltpu.make_async_copy(x_ref, o_ref.at[s, c], local_sem)
    own.start()
    for t in others:
        row = 2 * t + low
        remote(x_ref, o_ref.at[row, c], z_send.at[t], z_recv.at[t], {"sect": row}).wait_recv()
        send(o_ref.at[row, c], row, y_send.at[t], y_recv.at[t], across)
        send(o_ref.at[row, c], row, p_send.at[row], p_recv.at[row], partner)
    for t in [h] + others:
        row = 2 * t + 1 - low
        remote(x_ref, o_ref.at[row, c], y_send.at[t], y_recv.at[t], across).wait_recv()
        send(o_ref.at[row, c], row, p_send.at[row], p_recv.at[row], partner)
    for t in [h] + others:
        for row in (2 * t + low, 2 * t + 1 - low):
            remote(
                x_ref, o_ref.at[row, 1 - c], p_send.at[row], p_recv.at[row], partner
            ).wait_recv()
    own.wait()
    for copy in started:
        copy.wait_send()

def gather_rows(x, collective_id):
    sects = lax.axis_size("sect")
    heads = lax.axis_size("head")
    halves = sects // 2
    out = pl.pallas_call(
        gather_kernel,
        out_shape=jax.ShapeDtypeStruct((sects, heads) + x.shape, x.dtype),
        in_specs=[VMEM_SPEC],
        out_specs=VMEM_SPEC,
        scratch_shapes=[
            DMA((sects,)),
            DMA((sects,)),
            DMA((halves,)),
            DMA((halves,)),
            DMA((halves,)),
            DMA((halves,)),
            DMA,
        ],
        compiler_params=pltpu.CompilerParams(
            collective_id=collective_id, has_side_effects=True
        ),
        name="gather_rows",
    )(x)
    return out.reshape(-1, x.shape[1])

def reducer(place, mine, sect_of, p_ref, acc, rp, cs, ry, zs, rz, sems):
    s, c, h, low, halves, partner, across, others = place
    p_send, p_recv, y_send, y_recv, z_send, z_recv = sems

    def widen(x):
        return x.astype(jnp.float32)

    def to_partner(t, q, cut):
        return remote(
            p_ref.at[pl.ds(2 * t, 2), 1 - c, :, cut],
            rp.at[t, :, :, cut],
            p_send.at[0],
            p_recv.at[q, t],
            partner,
        )

    def to_across(t, q, cut):
        return remote(
            cs.at[t, :, cut], ry.at[t, :, cut], y_send.at[0], y_recv.at[q, t], across
        )

    def enter(t, q, cut):
        to_partner(t, q, cut).start()

    def cross(t, q, cut):
        to_partner(t, q, cut).wait_recv()
        cs[t, :, cut] = (
            widen(p_ref[2 * t + 1 - low, c, :, cut]) + widen(rp[t, 1 - low, :, cut])
        ).astype(jnp.bfloat16)
        to_across(t, q, cut).start()

    def along(t, q, cut):
        to_across(t, q, cut).wait_recv()
        total = (
            widen(p_ref[2 * t + low, c, :, cut])
            + widen(rp[t, low, :, cut])
            + widen(ry[t, :, cut])
        )
        if t is mine:
            acc[:, cut] = total
        else:
            zs[t, :, cut] = total.astype(jnp.bfloat16)
            remote(
                zs.at[t, :, cut],
                rz.at[mine, :, cut],
                z_send.at[0],
                z_recv.at[q, mine],
                {"sect": sect_of(t)},
            ).start()

    def collect(t, q, cut):
        if t is mine:
            return
        remote(
            zs.at[t, :, cut],
            rz.at[t, :, cut],
            z_send.at[0],
            z_recv.at[q, t],
            {"sect": sect_of(t)},
        ).wait_recv()
        acc[:, cut] += widen(rz[t, :, cut])

    def drain():
        remote(
            p_ref.at[:, 1 - c], p_ref.at[:, c], p_send.at[0], p_recv.at[0, 0], partner
        ).wait_send()
        remote(cs, ry, y_send.at[0], y_recv.at[0, 0], across).wait_send()
        some = pl.ds(0, cs.shape[0] - 1)
        remote(zs.at[some], rz.at[some], z_send.at[0], z_recv.at[0, 0], across).wait_send()

    return enter, cross, along, collect, drain

def layer_kernel(
    groups,
    sects,
    kv_heads,
    q_hbm,
    k_hbm,
    v_hbm,
    seg_hbm,
    proj_ref,
    res_hbm,
    gain_hbm,
    ids_hbm,
    route_hbm,
    gate_hbm,
    up_hbm,
    down_hbm,
    out_ref,
    q_ref,
    seg_ref,
    res_ref,
    gain_ref,
    ids_ref,
    route_ref,
    in_sems,
    gate_ref,
    up_ref,
    down_ref,
    hidden,
    xg,
    acc,
    p_first,
    p_second,
    rp_first,
    rp_second,
    first_bufs,
    cross_bufs,
    x_sems,
    tx_sems,
    rx_first,
    rx_second,
    z_second,
    w_sems,
    a_ref,
    w_all,
    kv_ref,
    kv_all,
    att,
    bias,
    kz_send,
    kz_recv,
    ky_send,
    ky_recv,
    a_send,
    a_recv,
    w_send,
    w_recv,
    f_send,
    f_recv,
    local_sem,
    own_w_sem,
    own_a_sem,
):
    place = positions()
    s, c, h, low, halves, partner, across, others = place
    g = lax.axis_index("groups")
    experts = lax.axis_size("sect") * lax.axis_size("head")
    moe_rows, width = res_ref.shape
    rows = q_ref.shape[0]
    chunk = 4 * moe_rows
    team = sects // 2
    line = team // 2
    j = lax.rem(s, team)
    base = s - j
    line_at = lax.rem(h, line)
    line_others = [lax.rem(line_at + i, line) for i in range(1, line)]
    sect_peers = [lax.rem(s + i, sects) for i in range(1, sects)]
    group_peers = [lax.rem(g + i, groups) for i in range(1, groups)]

    def teammate(i):
        return base + lax.rem(j + team + i, team)

    def opposite(i):
        return team - base + lax.rem(j + team + i, team)

    half = k_hbm.shape[1]
    own_k = pltpu.make_async_copy(k_hbm, kv_ref.at[:, pl.ds(0, half)], local_sem.at[0])
    own_v = pltpu.make_async_copy(v_hbm, kv_ref.at[:, pl.ds(half, half)], local_sem.at[1])
    own_k.start()
    own_v.start()
    inputs = [
        pltpu.make_async_copy(src, dst, in_sems.at[i])
        for i, (src, dst) in enumerate(
            (
                (seg_hbm, seg_ref),
                (q_hbm, q_ref),
                (res_hbm, res_ref),
                (gain_hbm, gain_ref),
                (ids_hbm, ids_ref),
                (route_hbm, route_ref),
            )
        )
    ]
    for copy in inputs:
        copy.start()
    greet(
        [{"sect": t} for t in sect_peers] + [{"groups": t} for t in group_peers] + [partner]
    )
    started = []

    def send(copy):
        copy.start()
        started.append(copy)

    own_k.wait()
    own_v.wait()

    window = bias.shape[1]
    blocks = window // rows
    first = jnp.maximum(s - (blocks - 1), 0)
    reach = min(blocks // 2, halves - 1)

    def kv_up(i):
        return remote(
            kv_ref, kv_all.at[s], kz_send.at[i], kz_recv.at[i], {"sect": s + 2 * i}
        )

    def kv_over(i):
        row = s - 2 * i
        return remote(
            kv_ref if i == 0 else kv_all.at[row],
            kv_all.at[row],
            ky_send.at[i],
            ky_recv.at[i],
            across,
        )

    for i in range(1, reach + 1):
        pl.when(h + i < halves)(kv_up(i).start)
    kv_over(0).start()
    own_kv = pltpu.make_async_copy(kv_ref, kv_all.at[s], local_sem.at[2])
    own_kv.start()

    pieces, w_rows, w_width = w_all.shape
    part = w_rows // groups
    w_cols = w_width // sects

    def w_piece(t, q):
        start = pl.multiple_of(lax.rem(t, team) * w_rows + g * part, part)
        return proj_ref.at[pl.ds(start, part), pl.ds(q * w_cols, w_cols)]

    def w_place(group, t, q):
        return w_all.at[
            q,
            pl.ds(pl.multiple_of(group * part, part), part),
            pl.ds(pl.multiple_of(t * w_cols, w_cols), w_cols),
        ]

    def w_side(group):
        return w_all.at[:, pl.ds(pl.multiple_of(group * part, part), part), :]

    def drain_weight():
        for i, u in enumerate(group_peers):
            remote(
                w_side(g), w_side(u), f_send.at[i], f_recv.at[g, 0], {"groups": u}
            ).wait_send()
        span = pl.ds(0, (sects - 1) * w_cols)
        side = w_all.at[:, pl.ds(0, part), span]
        remote(side, side, w_send.at[0], w_recv.at[0, 0], across).wait_send()

    def own_w(q):
        return pltpu.make_async_copy(w_piece(s, q), w_place(g, s, q), own_w_sem.at[q])

    def start_own(q):
        for i, u in enumerate(group_peers):
            remote(
                w_piece(s, q), w_place(g, s, q), f_send.at[i], f_recv.at[g, q], {"groups": u}
            ).start()
        own_w(q).start()

    def start_weight(q, targets):
        for t in targets:
            remote(
                w_piece(t, q), w_place(g, s, q), w_send.at[0], w_recv.at[q, s], {"sect": t}
            ).start()

    inside = [teammate(i) for i in range(1, team)]
    outside = [opposite(i) for i in range(team)]
    mixed = [outside[0]]
    for i in range(1, team):
        mixed += [inside[i - 1], outside[i]]
    ends = [jnp.where(base > 0, i, halves - 1 - i) for i in range(line)]
    far = [2 * z + y for z in ends for y in (low, 1 - low)]
    w_sources = far[:1] + [teammate(-i) for i in range(1, team)] + far[1:]

    def forward_weight(q, t):
        remote(
            w_piece(t, q), w_place(g, t, q), w_send.at[0], w_recv.at[q, t], {"sect": t}
        ).wait_recv()
        for i, u in enumerate(group_peers):
            remote(
                w_place(g, t, q), w_place(g, t, q), f_send.at[i], f_recv.at[g, q], {"groups": u}
            ).start()

    def wait_weight(q):
        for u in group_peers:
            remote(
                w_side(g).at[q], w_side(u).at[q], f_send.at[0], f_recv.at[u, q], {"groups": u}
            ).wait_recv()
        own_w(q).wait()

    loads = [
        pltpu.make_async_copy(src.at[0], dst, w_sems.at[i])
        for i, (src, dst) in enumerate(
            ((gate_hbm, gate_ref), (up_hbm, up_ref), (down_hbm, down_ref))
        )
    ]
    for load in loads:
        load.start()

    for q in range(pieces):
        start_own(q)
    start_weight(0, inside)
    start_weight(0, outside)
    for copy in inputs:
        copy.wait()
    row_of = lax.broadcasted_iota(jnp.int32, (rows, rows), 0)
    col_of = lax.broadcasted_iota(jnp.int32, (rows, rows), 1)
    seg_q = jnp.sum(
        jnp.where(row_of == col_of, seg_ref[s].astype(jnp.float32), 0.0), axis=1, keepdims=True
    )
    for b in range(blocks):
        behind = (s - first - b) * rows + row_of - col_of
        same = seg_q == seg_ref[first + b].astype(jnp.float32)
        bias[:, b * rows : (b + 1) * rows] = jnp.where(
            jnp.logical_and(same, behind >= 0), 0.0, MASKED
        )

        @pl.when(first + b > 2 * h + 1)
        def _(b=b):
            kv_all[first + b] = jnp.zeros(kv_all.shape[1:], kv_all.dtype)

    def relay_kv(i):
        remote(
            kv_ref, kv_all.at[s - 2 * i], kz_send.at[i], kz_recv.at[i], across
        ).wait_recv()
        kv_over(i).start()

    for i in range(1, reach + 1):
        pl.when(h - i >= 0)(functools.partial(relay_kv, i))

    def wait_kv(i):
        row = 2 * (h - i) + 1 - low
        remote(kv_ref, kv_all.at[row], ky_send.at[i], ky_recv.at[i], across).wait_recv()

    near = [teammate(-i) for i in range(1, team)]
    waiting = [(q, t) for q in range(pieces) for t in near]
    waiting += [(q, t) for q in range(pieces) for t in far]
    for i in range(reach + 1):
        pl.when(h - i >= 0)(functools.partial(wait_kv, i))
    if pieces > 1:
        start_weight(1, inside)
        start_weight(1, outside)
    own_kv.wait()

    scale = 1.0 / math.sqrt(HEAD_WIDTH)
    kv_width = kv_heads * HEAD_WIDTH
    per_kv = q_ref.shape[1] // kv_heads
    per, step_cols = att.shape[1], att.shape[3]
    cols = per * step_cols

    def attend(i):
        t = lax.rem(j + 1 + i // per, team)
        u = lax.rem(i, per)
        at = t * cols + u * step_cols
        kv_head = at // per_kv
        k_col = pl.multiple_of(kv_head * HEAD_WIDTH, HEAD_WIDTH)
        v_col = pl.multiple_of(kv_width + kv_head * HEAD_WIDTH, HEAD_WIDTH)
        span = pl.ds(first, blocks)
        keys = kv_all[span, :, pl.ds(k_col, HEAD_WIDTH)].reshape(window, HEAD_WIDTH)
        vals = kv_all[span, :, pl.ds(v_col, HEAD_WIDTH)].reshape(window, HEAD_WIDTH)
        for k in range(step_cols // HEAD_WIDTH):
            q_col = pl.multiple_of(at + k * HEAD_WIDTH, HEAD_WIDTH)
            q = q_ref[:, pl.ds(q_col, HEAD_WIDTH)]
            scores = lax.dot_general(
                q, keys, (((1,), (1,)), ((), ())), preferred_element_type=jnp.float32
            )
            scores = scores * scale + bias[...]
            top = jnp.max(scores, axis=1, keepdims=True)
            weights = jnp.exp(scores - top).astype(jnp.bfloat16)
            total = jnp.sum(weights.astype(jnp.float32), axis=1, keepdims=True)
            mixed = jnp.dot(weights, vals, preferred_element_type=jnp.float32)
            att[t, u, :, k * HEAD_WIDTH : (k + 1) * HEAD_WIDTH] = (mixed / total).astype(
                jnp.bfloat16
            )

    def a_place(t, u):
        return a_ref.at[
            pl.ds(pl.multiple_of(t * rows, rows), rows),
            pl.ds(pl.multiple_of(u * step_cols, step_cols), step_cols),
        ]

    def a_copy(t, u):
        return remote(
            att.at[t, u], a_place(j, u), a_send.at[0], a_recv.at[j, u], {"sect": base + t}
        )

    def step(i, carry):
        attend(i)
        last = i - 1

        @pl.when(jnp.logical_and(last >= 0, last < (team - 1) * per))
        def _():
            a_copy(lax.rem(j + 1 + last // per, team), lax.rem(last, per)).start()

        return carry

    steps = team * per
    segments = 4 if steps % 4 == 0 else 1
    for i in range(segments):
        lax.fori_loop(i * steps // segments, (i + 1) * steps // segments, step, 0)
        if i + 1 < segments:
            for _ in range(2):
                forward_weight(*waiting.pop(0))
    own_a = [
        pltpu.make_async_copy(att.at[j, u], a_place(j, u), own_a_sem.at[u]) for u in range(per)
    ]
    for copy in own_a:
        copy.start()
    while len(waiting) > (pieces - 1) * len(far):
        forward_weight(*waiting.pop(0))

    for _ in range(min(2, len(waiting))):
        forward_weight(*waiting.pop(0))
    team_peers = [lax.rem(j + i, team) for i in range(1, team)]
    for t in team_peers:
        for u in range(per):
            remote(
                att.at[t, u], a_place(t, u), a_send.at[0], a_recv.at[t, u], across
            ).wait_recv()
    for copy in own_a:
        copy.wait()

    tile = 512
    subs = 2 if w_width % (2 * tile) == 0 else 1

    def project(t, q, cut):
        left = a_ref[pl.ds(pl.multiple_of(t * chunk, chunk), chunk), :]
        which = cut.start // w_width
        for n in range(cut.start, cut.stop, tile):
            at = n - which * w_width
            part = jnp.dot(
                left, w_all[which, :, at : at + tile], preferred_element_type=jnp.float32
            )
            p_first[pl.ds(2 * t, 2), :, :, n : n + tile] = part.astype(jnp.bfloat16).reshape(
                2, 2, moe_rows, tile
            )

    enter, cross, along, collect, drain_first = reducer(
        place,
        line_at,
        lambda t: base + 2 * t + low,
        p_first,
        acc,
        rp_first,
        *[first_bufs.at[k] for k in range(4)],
        [tx_sems.at[pl.ds(0, 1)], rx_first.at[0]]
        + [tx_sems.at[pl.ds(1, 1)], rx_first.at[1]]
        + [tx_sems.at[pl.ds(2, 1)], rx_first.at[2]],
    )
    span = w_width // subs
    def cuts(q):
        return [
            (t, q * subs + i, slice(q * w_width + i * span, q * w_width + (i + 1) * span))
            for i in range(subs)
            for t in line_others + [line_at]
        ]

    behind = []
    for q in range(pieces):
        items = cuts(q)
        wait_weight(q)
        for i, item in enumerate(items):
            project(*item)
            enter(*item)
            if i >= 1 and q + 1 < pieces:
                cross(*items[i - 1])
        if q + 1 < pieces:
            cross(*items[-1])
            while waiting:
                forward_weight(*waiting.pop(0))
            behind += items
            continue
        n = len(behind)
        for i, item in enumerate(items):
            cross(*item)
            for other in behind[i * n // len(items) : (i + 1) * n // len(items)]:
                along(*other)
        for item in items:
            along(*item)
        for item in behind + items:
            collect(*item)

    summed = jnp.concatenate(
        [
            acc[:, q * w_width + t * w_cols : q * w_width + (t + 1) * w_cols]
            for t in range(sects)
            for q in range(pieces)
        ],
        axis=1,
    )
    mid = (res_ref[...].astype(jnp.float32) + summed).astype(jnp.bfloat16)
    out_ref[0] = mid
    wide = mid.astype(jnp.float32)
    inverse = lax.rsqrt(jnp.mean(wide * wide, axis=1, keepdims=True) + NORM_EPS)
    normed = wide * inverse * gain_ref[...].astype(jnp.float32).reshape(1, width)
    lanes = xg.shape[3] - width
    lane = lax.broadcasted_iota(jnp.int32, (moe_rows, lanes), 1)
    place_of = lax.broadcasted_iota(jnp.int32, (lanes, moe_rows), 0)
    route = route_ref[...]
    route = route / jnp.sum(route, axis=0, keepdims=True)
    share = jnp.zeros((lanes, moe_rows), jnp.float32)
    for k in range(route.shape[0]):
        ids = ids_ref[k : k + 1, :]
        named = jnp.logical_or(place_of == ids, place_of == ids + experts)
        share = share + jnp.where(named, route[k : k + 1, :], 0.0)
    share = share.T
    high = share.astype(jnp.bfloat16).astype(jnp.float32)
    xg[s, c, :, width:] = jnp.where(lane < experts, high, share - high).astype(jnp.bfloat16)
    xg[s, c, :, :width] = normed.astype(jnp.bfloat16)

    pg_send, pg_recv, yg_send, yg_recv, zg_send, zg_recv = [x_sems.at[j] for j in range(6)]

    def send_rows(row, send_sem, recv_sem, device):
        send(remote(xg.at[row, c], xg.at[row, c], send_sem, recv_sem, device))

    def arrived(row, core, recv_sem):
        remote(xg.at[row, core], xg.at[row, core], pg_send.at[row], recv_sem, partner).wait_recv()

    guarded = []

    def send_if(when, copy):
        pl.when(when)(copy.start)
        guarded.append((when, copy))

    def pass_up(t, slot):
        row = 2 * t + low
        return remote(
            xg.at[row, c], xg.at[row, c], zg_send.at[slot], zg_recv.at[t], {"sect": s + 2}
        )

    def pass_down(t, slot):
        row = 2 * t + low
        return remote(
            xg.at[row, c], xg.at[row, c], zg_send.at[slot], zg_recv.at[t], {"sect": s - 2}
        )

    paired = jnp.minimum(h, halves - 1 - h)
    away = jnp.where(2 * h < halves - 1, 1, -1)
    order = [h]
    hops = [0]
    for k in range(1, halves):
        near = (k + 1) // 2 * (-1 if k % 2 else 1)
        order.append(h + away * jnp.where(k <= 2 * paired, near, k - paired))
        hops.append(jnp.where(k <= 2 * paired, (k + 1) // 2, k - paired))

    def onward(k):
        t = order[k]
        row = 2 * t + low
        block = xg.at[row, c]
        return [
            (jnp.logical_and(t < h, h + 1 < halves), pass_up(t, t)),
            (jnp.logical_and(t > h, h >= 1), pass_down(t, t)),
        ], [
            remote(block, block, yg_send.at[t], yg_recv.at[t], across),
            remote(block, block, pg_send.at[row], pg_recv.at[row], partner),
        ]

    def relay_rows(k):
        t = order[k]
        arrived(2 * t + low, c, zg_recv.at[t])
        maybe, always = onward(k)
        for when, copy in maybe:
            pl.when(when)(copy.start)
        for copy in always:
            copy.start()

    for k in range(1, halves):
        maybe, always = onward(k)
        guarded.extend(maybe)
        started.extend(always)

    def relay_step(i):
        for k in range(i + 1, halves):
            if (k + 1) // 2 <= i + 1:
                pl.when(hops[k] == i + 1)(functools.partial(relay_rows, k))

    send_if(h + 1 < halves, pass_up(h, h))
    send_if(h >= 1, pass_down(h, halves + h))
    send_rows(s, yg_send.at[h], yg_recv.at[h], across)
    send_rows(s, pg_send.at[s], pg_recv.at[s], partner)
    for load in loads:
        load.wait()

    def experts_of(i, t, q, cut):
        if q == 0:
            hidden_of(i, t)
        for n in range(cut.start, cut.stop, tile):
            part = jnp.dot(
                hidden[...], down_ref[:, n : n + tile], preferred_element_type=jnp.float32
            )
            p_second[pl.ds(2 * t, 2), :, :, n : n + tile] = (
                (part * own_share(t)).astype(jnp.bfloat16).reshape(2, 2, moe_rows, tile)
            )

    def own_share(t):
        pair = xg[pl.ds(2 * t, 2), :, :, width:].astype(jnp.float32).reshape(chunk, lanes)
        expert = s * 2 + c
        at = lax.broadcasted_iota(jnp.int32, (chunk, lanes), 1)
        mine = jnp.logical_or(at == expert, at == expert + experts)
        return jnp.sum(jnp.where(mine, pair, 0.0), axis=1, keepdims=True)

    def hidden_of(i, t):
        relay_step(i)
        row = 2 * t + 1 - low
        arrived(row, c, yg_recv.at[t])
        send_rows(row, pg_send.at[row], pg_recv.at[row], partner)
        for row in (2 * t + low, 2 * t + 1 - low):
            arrived(row, 1 - c, pg_recv.at[row])
        x = xg[pl.ds(2 * t, 2), :, :, :width].reshape(chunk, width)
        step = 256
        for n in range(0, hidden.shape[1], step):
            gate_act = jnp.dot(
                x, gate_ref[:, n : n + step], preferred_element_type=jnp.float32
            )
            up_act = jnp.dot(x, up_ref[:, n : n + step], preferred_element_type=jnp.float32)
            silu = gate_act / (1.0 + jnp.exp(-gate_act))
            hidden[:, n : n + step] = (silu * up_act).astype(jnp.bfloat16)

    cs, ry, zs = [cross_bufs.at[k, pl.ds(0, halves)] for k in range(3)]
    rz = cross_bufs.at[3]
    y_send, y_recv = tx_sems.at[pl.ds(4, 1)], rx_second.at[1]
    z_send, z_recv = tx_sems.at[pl.ds(5, 1)], z_second
    sems = [tx_sems.at[pl.ds(3, 1)], rx_second.at[0], y_send, y_recv, z_send, z_recv]
    enter, cross, _, _, drain_second = reducer(
        place, h, None, p_second, acc, rp_second, cs, ry, zs, rz, sems
    )
    parts = 2 if width % 1024 == 0 else 1
    size = width // parts
    cuts_of = [(q, slice(q * size, (q + 1) * size)) for q in range(parts)]

    def own_sum(t, q, cut):
        return (
            p_second[2 * t + low, c, :, cut].astype(jnp.float32)
            + rp_second[t, low, :, cut].astype(jnp.float32)
            + ry[t, :, cut].astype(jnp.float32)
        )

    def wait_across(t, q, cut):
        remote(
            cs.at[t, :, cut], ry.at[t, :, cut], y_send.at[0], y_recv.at[q, t], across
        ).wait_recv()

    def wait_along(slot, row, t, q, cut):
        remote(
            zs.at[t, :, cut], rz.at[slot, :, cut], z_send.at[0], z_recv.at[row, t], across
        ).wait_recv()

    def chain(t, q, cut):
        wait_across(t, q, cut)
        joined = jnp.where(t > h, h >= 1, h + 1 < halves)

        @pl.when(jnp.logical_not(joined))
        def _():
            zs[t, :, cut] = own_sum(t, q, cut).astype(jnp.bfloat16)

        @pl.when(joined)
        def _():
            wait_along(t, q, t, q, cut)
            zs[t, :, cut] = (
                own_sum(t, q, cut) + rz[t, :, cut].astype(jnp.float32)
            ).astype(jnp.bfloat16)

        landed = h - 1 == t
        remote(
            zs.at[t, :, cut],
            rz.at[jnp.where(landed, halves, t), :, cut],
            z_send.at[0],
            z_recv.at[q + jnp.where(landed, parts, 0), t],
            {"sect": s + jnp.where(t > h, 2, -2)},
        ).start()

    def finish(q, cut):
        wait_across(h, q, cut)
        acc[:, cut] = own_sum(h, q, cut)

        @pl.when(h >= 1)
        def _():
            wait_along(h, q, h, q, cut)
            acc[:, cut] += rz[h, :, cut].astype(jnp.float32)

        @pl.when(h + 1 < halves)
        def _():
            wait_along(halves, q + parts, h, q, cut)
            acc[:, cut] += rz[halves, :, cut].astype(jnp.float32)

    lower = h < halves // 2
    targets = [
        jnp.where(lower, halves // 2 + i, halves // 2 - 1 - i) for i in range(halves // 2)
    ]
    targets += [h - line_at + t for t in line_others]

    def each(step, t):
        for q, cut in cuts_of:
            step(t, q, cut)

    for i, t in enumerate(order):
        for q, cut in cuts_of:
            experts_of(i, t, q, cut)
            enter(t, q, cut)
        if i == halves - 2:
            each(cross, targets[0])
    for i, t in enumerate(targets[1:] + [h]):
        each(cross, t)
        if i < 0:
            each(chain, targets[i])
    for t in targets[0:]:
        each(chain, t)
    for q, cut in cuts_of:
        finish(q, cut)
    out_ref[1] = acc[...].astype(jnp.bfloat16)
    for i in range(1, reach + 1):
        pl.when(h + i < halves)(kv_up(i).wait_send)
    for i in range(reach + 1):
        pl.when(h - i >= 0)(kv_over(i).wait_send)
    some = pl.ds(0, team - 1)
    remote(att.at[some], att.at[some], a_send.at[0], a_recv.at[0, 0], across).wait_send()
    drain_weight()
    drain_first()
    drain_second()
    for when, copy in guarded:
        pl.when(when)(copy.wait_send)
    for copy in started:
        copy.wait_send()

def fused_layer(
    queries, keys, values, segments, proj, residual, gain, ids, route, gate, up, down
):
    groups = lax.axis_size("groups")
    sects = lax.axis_size("sect")
    heads = lax.axis_size("head")
    rows = queries.shape[0]
    team = sects // 2
    cols = queries.shape[1] // team
    step_cols = min(cols, 4 * HEAD_WIDTH)
    per = cols // step_cols
    pieces = 2 if proj.shape[1] % 256 == 0 else 1
    w_rows = proj.shape[0] // team
    blocks = min(sects, -(-segments.shape[0] // (2 * rows)) + 1)
    halves = sects // 2
    block = residual.shape
    lanes = -(-2 * sects * heads // 128) * 128
    bf16 = jnp.bfloat16
    kv_shape = (rows, 2 * keys.shape[1])
    operands = (
        queries,
        keys,
        values,
        segments.reshape(sects, 1, rows),
        proj,
        residual,
        gain,
        ids.T,
        route.T,
        gate,
        up,
        down,
    )
    both = pl.pallas_call(
        functools.partial(layer_kernel, groups, sects, keys.shape[1] // HEAD_WIDTH),
        out_shape=jax.ShapeDtypeStruct((2,) + block, bf16),
        in_specs=[pl.BlockSpec(memory_space=pltpu.HBM)] * len(operands),
        out_specs=VMEM_SPEC,
        scratch_shapes=[
            pltpu.VMEM(queries.shape, bf16),
            pltpu.VMEM((sects, 1, rows), jnp.int32),
            pltpu.VMEM(block, bf16),
            pltpu.VMEM(gain.shape, bf16),
            pltpu.VMEM(ids.shape[::-1], jnp.int32),
            pltpu.VMEM(route.shape[::-1], jnp.float32),
            DMA((6,)),
            pltpu.VMEM(gate.shape[1:], bf16),
            pltpu.VMEM(up.shape[1:], bf16),
            pltpu.VMEM(down.shape[1:], bf16),
            pltpu.VMEM((4 * block[0], gate.shape[2]), bf16),
            pltpu.VMEM((sects, heads, block[0], block[1] + lanes), bf16),
            pltpu.VMEM(block, jnp.float32),
            pltpu.VMEM((team, heads) + block, bf16),
            pltpu.VMEM((sects, heads) + block, bf16),
            pltpu.VMEM((team // 2, 2) + block, bf16),
            pltpu.VMEM((halves, 2) + block, bf16),
            pltpu.VMEM((4, team // 2) + block, bf16),
            pltpu.VMEM((4, halves + 1) + block, bf16),
            DMA((6, sects)),
            DMA((6,)),
            DMA((3, 2 * pieces, team // 2)),
            DMA((2, 2, halves)),
            DMA((4, halves)),
            DMA((3,)),
            pltpu.VMEM((rows * team, cols), bf16),
            pltpu.VMEM((pieces, w_rows, proj.shape[1] // pieces * sects), bf16),
            pltpu.VMEM(kv_shape, bf16),
            pltpu.VMEM((sects,) + kv_shape, bf16),
            pltpu.VMEM((team, per, rows, step_cols), bf16),
            pltpu.VMEM((rows, blocks * rows), jnp.float32),
            DMA((halves,)),
            DMA((halves,)),
            DMA((halves,)),
            DMA((halves,)),
            DMA((1,)),
            DMA((team, per)),
            DMA((1,)),
            DMA((pieces, sects)),
            DMA((groups,)),
            DMA((groups, pieces)),
            DMA((3,)),
            DMA((pieces,)),
            DMA((per,)),
        ],
        compiler_params=pltpu.CompilerParams(
            collective_id=4, has_side_effects=True, vmem_limit_bytes=LAYER_ROOM
        ),
        name="layer",
    )(*[pltpu.with_memory_space_constraint(x, pltpu.HBM) for x in operands])
    return both[0], both[1]

def shards(
    queries,
    packed_key_rows,
    values,
    segments,
    proj_weight,
    residual,
    norm_gain,
    expert_ids,
    route_weights,
    gate_weight,
    up_weight,
    down_weight,
):
    sects = lax.axis_size("sect")
    heads = lax.axis_size("head")
    s = lax.axis_index("sect")
    c = lax.axis_index("head")
    experts = sects * heads
    moe_rows, width = residual.shape
    fits = experts * moe_rows * width * 24 <= VMEM_ROOM
    if fits and sects % 4 == 0 and proj_weight.shape[1] % 128 == 0:
        return fused_layer(
            queries,
            packed_key_rows,
            values,
            segments,
            proj_weight,
            residual,
            norm_gain,
            expert_ids,
            route_weights,
            gate_weight,
            up_weight,
            down_weight,
        )
    attended, weight = exchange_attention(
        queries, packed_key_rows, values, segments, proj_weight
    )
    partial_rows = jnp.dot(attended, weight, preferred_element_type=jnp.float32)
    projected = sum_scatter(partial_rows.astype(jnp.bfloat16), moe_rows, 1)

    hidden_mid = (residual.astype(jnp.float32) + projected).astype(jnp.bfloat16)
    mid_float = lax.optimization_barrier(hidden_mid).astype(jnp.float32)
    inverse = lax.rsqrt(jnp.mean(mid_float * mid_float, axis=1, keepdims=True) + NORM_EPS)
    normed = (mid_float * inverse * norm_gain.astype(jnp.float32)[None, :]).astype(jnp.bfloat16)

    route_share = route_weights / jnp.sum(route_weights, axis=1, keepdims=True)
    named = expert_ids[:, :, None] == jnp.arange(experts, dtype=jnp.int32)[None, None, :]
    share = jnp.sum(jnp.where(named, route_share[:, :, None], 0.0), axis=1)
    share_high = lax.reduce_precision(share, 8, 7)
    share_low = (share - share_high).astype(jnp.bfloat16)
    pad = -(2 * experts) % 128
    sent = jnp.concatenate(
        [
            normed,
            share_high.astype(jnp.bfloat16),
            share_low,
            jnp.zeros((moe_rows, pad), jnp.bfloat16),
        ],
        axis=1,
    )
    gathered = gather_rows(sent, 2)
    expert = s * heads + c
    all_rows = gathered[:, :width]
    pair = gathered[:, width:].astype(jnp.float32)
    lane = jnp.arange(pair.shape[1], dtype=jnp.int32)[None, :]
    mine = jnp.logical_or(lane == expert, lane == expert + experts)
    own_share = jnp.sum(jnp.where(mine, pair, 0.0), axis=1, keepdims=True)
    gate_act = jnp.dot(all_rows, gate_weight[0], preferred_element_type=jnp.float32)
    up_act = jnp.dot(all_rows, up_weight[0], preferred_element_type=jnp.float32)
    hidden = (jax.nn.silu(gate_act) * up_act).astype(jnp.bfloat16)
    result = jnp.dot(hidden, down_weight[0], preferred_element_type=jnp.float32)
    mixed = (result * own_share).astype(jnp.bfloat16)
    mixture = sum_scatter(mixed, moe_rows, 3)
    return (hidden_mid, mixture.astype(jnp.bfloat16))

def solution(mesh):
    rows = P(("groups", "sect", "head"), None)
    split = P(("groups", "sect"), "head")
    expert = P(("sect", "head"), None, None)
    placed = (
        split,
        split,
        split,
        P("groups"),
        P("head", "sect"),
        rows,
        P(),
        rows,
        rows,
        expert,
        expert,
        expert,
    )
    return jax.shard_map(
        shards, mesh=mesh, in_specs=placed, out_specs=(rows, rows), check_vma=False
    )
```

profile of v0, /device:TPU:0, one launch (start us, length us, event | category | flops | bytes accessed | tf_op | source)
XLA Modules:
  0.0 136.7 jit_solution(644211971050606111)
XLA Ops:
  0.6 135.2 %layer.1 = bf16[2,64,2048]{2,1,0:T(8,128)(2,1)S(1)} custom-call(bf16[128,4096]{1,0:T(8,128)(2,1)} %q_hbm.1, bf16[128,256]{1,0:T(8,128)(2,1)} %k_hbm.1, bf16[128,256]{1,0:T(8,128)(2,1)} %v_hbm.1, s32[8,1,128]{2,1,0:T(1,128)} %bitcast.7, bf16[4096,256]{1,0:T(8,128)(2,1)} %proj_ref.1, bf16[64,2048]{1,0:T(8,128)(2,1)} %res_hbm.1, bf16[2048]{0:T(1024)(128)(2,1)} %gain_hbm.1, ...), custom_call_target="tpu_custom_call" | custom-call | tf_op jit(solution)/shard_map/layer/pallas_call | solution.py:1195
  135.8 0.8 slice_bitcast_fusion
where the time goes:
time: 137 us
  Pallas kernels  135 us (99%)
    pallas_call x1, Pallas kernels, fused_layer(): pl.pallas_call(functools.partial(layer_kernel, groups, sects, keys.shape[...  135 us

commit v1 on v0

--- a/solution.py
+++ b/solution.py
@@ -551,7 +551,11 @@
     rp_second,
     first_bufs,
     cross_bufs,
-    x_sems,
+    row_tx,
+    row_pair,
+    row_over,
+    row_tx_along,
+    row_along,
     tx_sems,
     rx_first,
     rx_second,
@@ -945,31 +949,33 @@
     xg[s, c, :, width:] = jnp.where(lane < experts, high, share - high).astype(jnp.bfloat16)
     xg[s, c, :, :width] = normed.astype(jnp.bfloat16)
 
-    pg_send, pg_recv, yg_send, yg_recv, zg_send, zg_recv = [x_sems.at[j] for j in range(6)]
-
-    def send_rows(row, send_sem, recv_sem, device):
-        send(remote(xg.at[row, c], xg.at[row, c], send_sem, recv_sem, device))
-
-    def arrived(row, core, recv_sem):
-        remote(xg.at[row, core], xg.at[row, core], pg_send.at[row], recv_sem, partner).wait_recv()
-
     guarded = []
-
-    def send_if(when, copy):
-        pl.when(when)(copy.start)
-        guarded.append((when, copy))
-
-    def pass_up(t, slot):
-        row = 2 * t + low
+    total = xg.shape[3]
+    middle = total // 256 * 128
+    row_cuts = [slice(0, middle), slice(middle, total)]
+
+    def hop(t, p, slot, step):
+        block = xg.at[2 * t + low, c, :, row_cuts[p]]
         return remote(
-            xg.at[row, c], xg.at[row, c], zg_send.at[slot], zg_recv.at[t], {"sect": s + 2}
-        )
-
-    def pass_down(t, slot):
-        row = 2 * t + low
-        return remote(
-            xg.at[row, c], xg.at[row, c], zg_send.at[slot], zg_recv.at[t], {"sect": s - 2}
-        )
+            block, block, row_tx_along.at[p, slot], row_along.at[p, t], {"sect": s + step}
+        )
+
+    def over(t, p):
+        block = xg.at[2 * t + low, c, :, row_cuts[p]]
+        return remote(block, block, row_tx.at[0], row_over.at[p, t], across)
+
+    def to_pair(row):
+        block = xg.at[row, c]
+        remote(block, block, row_tx.at[1], row_pair.at[row], partner).start()
+
+    def from_pair(row):
+        block = xg.at[row, 1 - c]
+        remote(block, block, row_tx.at[1], row_pair.at[row], partner).wait_recv()
+
+    def from_over(t):
+        for p, cut in enumerate(row_cuts):
+            block = xg.at[2 * t + 1 - low, c, :, cut]
+            remote(block, block, row_tx.at[0], row_over.at[p, t], across).wait_recv()
 
     paired = jnp.minimum(h, halves - 1 - h)
     away = jnp.where(2 * h < halves - 1, 1, -1)
@@ -980,41 +986,43 @@
         order.append(h + away * jnp.where(k <= 2 * paired, near, k - paired))
         hops.append(jnp.where(k <= 2 * paired, (k + 1) // 2, k - paired))
 
-    def onward(k):
+    def onward(k, p):
         t = order[k]
-        row = 2 * t + low
-        block = xg.at[row, c]
         return [
-            (jnp.logical_and(t < h, h + 1 < halves), pass_up(t, t)),
-            (jnp.logical_and(t > h, h >= 1), pass_down(t, t)),
-        ], [
-            remote(block, block, yg_send.at[t], yg_recv.at[t], across),
-            remote(block, block, pg_send.at[row], pg_recv.at[row], partner),
+            (jnp.logical_and(t < h, h + 1 < halves), hop(t, p, t, 2)),
+            (jnp.logical_and(t > h, h >= 1), hop(t, p, t, -2)),
         ]
 
     def relay_rows(k):
         t = order[k]
-        arrived(2 * t + low, c, zg_recv.at[t])
-        maybe, always = onward(k)
-        for when, copy in maybe:
-            pl.when(when)(copy.start)
-        for copy in always:
-            copy.start()
+        for p in range(2):
+            block = xg.at[2 * t + low, c, :, row_cuts[p]]
+            remote(
+                block, block, row_tx_along.at[p, t], row_along.at[p, t], across
+            ).wait_recv()
+            for when, copy in onward(k, p):
+                pl.when(when)(copy.start)
+            over(t, p).start()
+        to_pair(2 * t + low)
 
     for k in range(1, halves):
-        maybe, always = onward(k)
-        guarded.extend(maybe)
-        started.extend(always)
+        for p in range(2):
+            guarded.extend(onward(k, p))
 
     def relay_step(i):
         for k in range(i + 1, halves):
             if (k + 1) // 2 <= i + 1:
                 pl.when(hops[k] == i + 1)(functools.partial(relay_rows, k))
 
-    send_if(h + 1 < halves, pass_up(h, h))
-    send_if(h >= 1, pass_down(h, halves + h))
-    send_rows(s, yg_send.at[h], yg_recv.at[h], across)
-    send_rows(s, pg_send.at[s], pg_recv.at[s], partner)
+    for p in range(2):
+        for when, copy in (
+            (h + 1 < halves, hop(h, p, h, 2)),
+            (h >= 1, hop(h, p, halves + h, -2)),
+        ):
+            pl.when(when)(copy.start)
+            guarded.append((when, copy))
+        over(h, p).start()
+    to_pair(s)
     for load in loads:
         load.wait()
 
@@ -1038,11 +1046,10 @@
 
     def hidden_of(i, t):
         relay_step(i)
-        row = 2 * t + 1 - low
-        arrived(row, c, yg_recv.at[t])
-        send_rows(row, pg_send.at[row], pg_recv.at[row], partner)
+        from_over(t)
+        to_pair(2 * t + 1 - low)
         for row in (2 * t + low, 2 * t + 1 - low):
-            arrived(row, 1 - c, pg_recv.at[row])
+            from_pair(row)
         x = xg[pl.ds(2 * t, 2), :, :, :width].reshape(chunk, width)
         step = 256
         for n in range(0, hidden.shape[1], step):
@@ -1151,6 +1158,10 @@
         pl.when(h - i >= 0)(kv_over(i).wait_send)
     some = pl.ds(0, team - 1)
     remote(att.at[some], att.at[some], a_send.at[0], a_recv.at[0, 0], across).wait_send()
+    rows_sent = xg.at[pl.ds(0, halves), c]
+    remote(rows_sent, rows_sent, row_tx.at[0], row_over.at[0, 0], across).wait_send()
+    rows_sent = xg.at[:, c]
+    remote(rows_sent, rows_sent, row_tx.at[1], row_pair.at[0], partner).wait_send()
     drain_weight()
     drain_first()
     drain_second()
@@ -1217,7 +1228,11 @@
             pltpu.VMEM((halves, 2) + block, bf16),
             pltpu.VMEM((4, team // 2) + block, bf16),
             pltpu.VMEM((4, halves + 1) + block, bf16),
-            DMA((6, sects)),
+            DMA((2,)),
+            DMA((sects,)),
+            DMA((2, halves)),
+            DMA((2, sects)),
+            DMA((2, halves)),
             DMA((6,)),
             DMA((3, 2 * pieces, team // 2)),
             DMA((2, 2, halves)),

time: 137 us -> 138 us (level)
  no operation moved by 1% of the time
where the time goes in v1:
time: 138 us
  Pallas kernels  136 us (99%)
    pallas_call x1, Pallas kernels, fused_layer(): pl.pallas_call(functools.partial(layer_kernel, groups, sects, keys.shape[...  136 us

profile of v1, /device:TPU:0, one launch (start us, length us, event | category | flops | bytes accessed | tf_op | source)
XLA Modules:
  0.0 137.6 jit_solution(11986726238938654524)
XLA Ops:
  0.6 136.1 %layer.1 = bf16[2,64,2048]{2,1,0:T(8,128)(2,1)S(1)} custom-call(bf16[128,4096]{1,0:T(8,128)(2,1)} %q_hbm.1, bf16[128,256]{1,0:T(8,128)(2,1)} %k_hbm.1, bf16[128,256]{1,0:T(8,128)(2,1)} %v_hbm.1, s32[8,1,128]{2,1,0:T(1,128)} %bitcast.7, bf16[4096,256]{1,0:T(8,128)(2,1)} %proj_ref.1, bf16[64,2048]{1,0:T(8,128)(2,1)} %res_hbm.1, bf16[2048]{0:T(1024)(128)(2,1)} %gain_hbm.1, ...), custom_call_target="tpu_custom_call" | custom-call | tf_op jit(solution)/shard_map/layer/pallas_call | solution.py:1206
  136.8 0.8 slice_bitcast_fusion

commit v2 on v1

--- a/solution.py
+++ b/solution.py
@@ -669,20 +669,27 @@
         start = pl.multiple_of(lax.rem(t, team) * w_rows + g * part, part)
         return proj_ref.at[pl.ds(start, part), pl.ds(q * w_cols, w_cols)]
 
-    def w_place(group, t, q):
+    def w_place(group, t, q, home=base):
         return w_all.at[
             q,
             pl.ds(pl.multiple_of(group * part, part), part),
-            pl.ds(pl.multiple_of(t * w_cols, w_cols), w_cols),
+            pl.ds(pl.multiple_of(lax.rem(t - home + sects, sects) * w_cols, w_cols), w_cols),
         ]
 
     def w_side(group):
         return w_all.at[:, pl.ds(pl.multiple_of(group * part, part), part), :]
+
+    def w_half(group, q, which):
+        return w_all.at[
+            q,
+            pl.ds(pl.multiple_of(group * part, part), part),
+            pl.ds(which * team * w_cols, team * w_cols),
+        ]
 
     def drain_weight():
         for i, u in enumerate(group_peers):
             remote(
-                w_side(g), w_side(u), f_send.at[i], f_recv.at[g, 0], {"groups": u}
+                w_side(g), w_side(u), f_send.at[i], f_recv.at[g, 0, 0], {"groups": u}
             ).wait_send()
         span = pl.ds(0, (sects - 1) * w_cols)
         side = w_all.at[:, pl.ds(0, part), span]
@@ -694,14 +701,18 @@
     def start_own(q):
         for i, u in enumerate(group_peers):
             remote(
-                w_piece(s, q), w_place(g, s, q), f_send.at[i], f_recv.at[g, q], {"groups": u}
+                w_piece(s, q), w_place(g, s, q), f_send.at[i], f_recv.at[g, q, 0], {"groups": u}
             ).start()
         own_w(q).start()
 
     def start_weight(q, targets):
         for t in targets:
             remote(
-                w_piece(t, q), w_place(g, s, q), w_send.at[0], w_recv.at[q, s], {"sect": t}
+                w_piece(t, q),
+                w_place(g, s, q, t - lax.rem(t, team)),
+                w_send.at[0],
+                w_recv.at[q, s],
+                {"sect": t},
             ).start()
 
     inside = [teammate(i) for i in range(1, team)]
@@ -713,21 +724,36 @@
     far = [2 * z + y for z in ends for y in (low, 1 - low)]
     w_sources = far[:1] + [teammate(-i) for i in range(1, team)] + far[1:]
 
+    near = [teammate(-i) for i in range(1, team)]
+
+    def inner(t):
+        return int(any(t is u for u in near))
+
     def forward_weight(q, t):
+        which = 1 - inner(t)
         remote(
             w_piece(t, q), w_place(g, t, q), w_send.at[0], w_recv.at[q, t], {"sect": t}
         ).wait_recv()
         for i, u in enumerate(group_peers):
             remote(
-                w_place(g, t, q), w_place(g, t, q), f_send.at[i], f_recv.at[g, q], {"groups": u}
+                w_place(g, t, q),
+                w_place(g, t, q),
+                f_send.at[i],
+                f_recv.at[g, q, which],
+                {"groups": u},
             ).start()
 
-    def wait_weight(q):
+    def wait_weight(q, which):
         for u in group_peers:
             remote(
-                w_side(g).at[q], w_side(u).at[q], f_send.at[0], f_recv.at[u, q], {"groups": u}
+                w_half(g, q, which),
+                w_half(u, q, which),
+                f_send.at[0],
+                f_recv.at[u, q, which],
+                {"groups": u},
             ).wait_recv()
-        own_w(q).wait()
+        if which == 0:
+            own_w(q).wait()
 
     loads = [
         pltpu.make_async_copy(src.at[0], dst, w_sems.at[i])
@@ -773,7 +799,6 @@
         row = 2 * (h - i) + 1 - low
         remote(kv_ref, kv_all.at[row], ky_send.at[i], ky_recv.at[i], across).wait_recv()
 
-    near = [teammate(-i) for i in range(1, team)]
     waiting = [(q, t) for q in range(pieces) for t in near]
     waiting += [(q, t) for q in range(pieces) for t in far]
     for i in range(reach + 1):
@@ -861,20 +886,18 @@
     for copy in own_a:
         copy.wait()
 
-    tile = 512
-    subs = 2 if w_width % (2 * tile) == 0 else 1
+    span = team * w_cols
 
     def project(t, q, cut):
         left = a_ref[pl.ds(pl.multiple_of(t * chunk, chunk), chunk), :]
         which = cut.start // w_width
-        for n in range(cut.start, cut.stop, tile):
-            at = n - which * w_width
-            part = jnp.dot(
-                left, w_all[which, :, at : at + tile], preferred_element_type=jnp.float32
-            )
-            p_first[pl.ds(2 * t, 2), :, :, n : n + tile] = part.astype(jnp.bfloat16).reshape(
-                2, 2, moe_rows, tile
-            )
+        at = cut.start - which * w_width
+        part = jnp.dot(
+            left, w_all[which, :, at : at + span], preferred_element_type=jnp.float32
+        )
+        p_first[pl.ds(2 * t, 2), :, :, cut] = part.astype(jnp.bfloat16).reshape(
+            2, 2, moe_rows, span
+        )
 
     enter, cross, along, collect, drain_first = reducer(
         place,
@@ -888,47 +911,60 @@
         + [tx_sems.at[pl.ds(1, 1)], rx_first.at[1]]
         + [tx_sems.at[pl.ds(2, 1)], rx_first.at[2]],
     )
-    span = w_width // subs
-    def cuts(q):
-        return [
-            (t, q * subs + i, slice(q * w_width + i * span, q * w_width + (i + 1) * span))
-            for i in range(subs)
-            for t in line_others + [line_at]
-        ]
-
-    behind = []
-    for q in range(pieces):
-        items = cuts(q)
-        wait_weight(q)
+    def items_of(q, which):
+        start = q * w_width + which * span
+        cut = slice(start, start + span)
+        return [(t, 2 * q + which, cut) for t in line_others + [line_at]]
+
+    def begin(items):
         for i, item in enumerate(items):
             project(*item)
             enter(*item)
-            if i >= 1 and q + 1 < pieces:
-                cross(*items[i - 1])
+
+    def forward(count):
+        for _ in range(min(count, len(waiting))):
+            forward_weight(*waiting.pop(0))
+
+    behind = []
+    for q in range(pieces):
+        wait_weight(q, 0)
+        behind += items_of(q, 0)
+    begin(behind)
+    for item in behind:
+        cross(*item)
+    forward(1)
+    for q in range(pieces):
+        if q + 1 == pieces:
+            forward(len(waiting))
+        items = items_of(q, 1)
+        wait_weight(q, 1)
+        begin(items)
         if q + 1 < pieces:
-            cross(*items[-1])
-            while waiting:
-                forward_weight(*waiting.pop(0))
+            for item in items:
+                cross(*item)
             behind += items
-            continue
-        n = len(behind)
-        for i, item in enumerate(items):
-            cross(*item)
-            for other in behind[i * n // len(items) : (i + 1) * n // len(items)]:
-                along(*other)
-        for item in items:
-            along(*item)
-        for item in behind + items:
-            collect(*item)
-
-    summed = jnp.concatenate(
-        [
-            acc[:, q * w_width + t * w_cols : q * w_width + (t + 1) * w_cols]
-            for t in range(sects)
-            for q in range(pieces)
-        ],
-        axis=1,
-    )
+    n = len(behind)
+    for i, item in enumerate(items):
+        cross(*item)
+        for other in behind[i * n // len(items) : (i + 1) * n // len(items)]:
+            along(*other)
+    for item in items:
+        along(*item)
+    for item in behind + items:
+        collect(*item)
+
+    def columns(swap):
+        order = [(t + swap) % sects for t in range(sects)]
+        return jnp.concatenate(
+            [
+                acc[:, q * w_width + t * w_cols : q * w_width + (t + 1) * w_cols]
+                for t in order
+                for q in range(pieces)
+            ],
+            axis=1,
+        )
+
+    summed = jnp.where(base == 0, columns(0), columns(team))
     mid = (res_ref[...].astype(jnp.float32) + summed).astype(jnp.bfloat16)
     out_ref[0] = mid
     wide = mid.astype(jnp.float32)
@@ -1029,6 +1065,7 @@
     def experts_of(i, t, q, cut):
         if q == 0:
             hidden_of(i, t)
+        tile = min(512, width)
         for n in range(cut.start, cut.stop, tile):
             part = jnp.dot(
                 hidden[...], down_ref[:, n : n + tile], preferred_element_type=jnp.float32
@@ -1253,7 +1290,7 @@
             DMA((1,)),
             DMA((pieces, sects)),
             DMA((groups,)),
-            DMA((groups, pieces)),
+            DMA((groups, pieces, 2)),
             DMA((3,)),
             DMA((pieces,)),
             DMA((per,)),

time: 138 us -> 136 us (0.986)
  Pallas kernels: 136 us -> 134 us
    pallas_call x1, Pallas kernels: 136 us -> 134 us  [fused_layer(): pl.pallas_call(functools.partial(layer_kernel, groups, sects, keys.shape[...]
where the time goes in v2:
time: 136 us
  Pallas kernels  134 us (99%)
    pallas_call x1, Pallas kernels, fused_layer(): pl.pallas_call(functools.partial(layer_kernel, groups, sects, keys.shape[...  134 us

profile of v2, /device:TPU:0, one launch (start us, length us, event | category | flops | bytes accessed | tf_op | source)
XLA Modules:
  0.0 135.7 jit_solution(3992718264710591975)
XLA Ops:
  0.6 134.2 %layer.1 = bf16[2,64,2048]{2,1,0:T(8,128)(2,1)S(1)} custom-call(bf16[128,4096]{1,0:T(8,128)(2,1)} %q_hbm.1, bf16[128,256]{1,0:T(8,128)(2,1)} %k_hbm.1, bf16[128,256]{1,0:T(8,128)(2,1)} %v_hbm.1, s32[8,1,128]{2,1,0:T(1,128)} %bitcast.7, bf16[4096,256]{1,0:T(8,128)(2,1)} %proj_ref.1, bf16[64,2048]{1,0:T(8,128)(2,1)} %res_hbm.1, bf16[2048]{0:T(1024)(128)(2,1)} %gain_hbm.1, ...), custom_call_target="tpu_custom_call" | custom-call | tf_op jit(solution)/shard_map/layer/pallas_call | solution.py:1243
  134.8 0.8 slice_bitcast_fusion

commit v3 on v2

--- a/solution.py
+++ b/solution.py
@@ -875,7 +875,7 @@
     while len(waiting) > (pieces - 1) * len(far):
         forward_weight(*waiting.pop(0))
 
-    for _ in range(min(2, len(waiting))):
+    for _ in range(min(3, len(waiting))):
         forward_weight(*waiting.pop(0))
     team_peers = [lax.rem(j + i, team) for i in range(1, team)]
     for t in team_peers:

time: 136 us -> 134 us (0.985)
  Pallas kernels: 134 us -> 132 us
    pallas_call x1, Pallas kernels: 134 us -> 132 us  [fused_layer(): pl.pallas_call(functools.partial(layer_kernel, groups, sects, keys.shape[...]
where the time goes in v3:
time: 134 us
  Pallas kernels  132 us (99%)
    pallas_call x1, Pallas kernels, fused_layer(): pl.pallas_call(functools.partial(layer_kernel, groups, sects, keys.shape[...  132 us

profile of v3, /device:TPU:0, one launch (start us, length us, event | category | flops | bytes accessed | tf_op | source)
XLA Modules:
  0.0 133.9 jit_solution(10567256609017563137)
XLA Ops:
  0.6 132.4 %layer.1 = bf16[2,64,2048]{2,1,0:T(8,128)(2,1)S(1)} custom-call(bf16[128,4096]{1,0:T(8,128)(2,1)} %q_hbm.1, bf16[128,256]{1,0:T(8,128)(2,1)} %k_hbm.1, bf16[128,256]{1,0:T(8,128)(2,1)} %v_hbm.1, s32[8,1,128]{2,1,0:T(1,128)} %bitcast.7, bf16[4096,256]{1,0:T(8,128)(2,1)} %proj_ref.1, bf16[64,2048]{1,0:T(8,128)(2,1)} %res_hbm.1, bf16[2048]{0:T(1024)(128)(2,1)} %gain_hbm.1, ...), custom_call_target="tpu_custom_call" | custom-call | tf_op jit(solution)/shard_map/layer/pallas_call | solution.py:1243
  133.0 0.8 slice_bitcast_fusion
